TPU v7x, 32 devices: a whole 2x2x4 slice. The times are simulated.
32 devices in a mesh: pair: 16 (over z, y, x), dp: 2 (over core).
Axes of the slice: x: 2, y: 2, z: 4, core: 2. Of those that a mesh axis runs over, the one named last changes fastest.
Arguments:
- features: bfloat16 [16384, 2048], P(('pair', 'dp')), may hold values from -6 to 6
- proj_weight: bfloat16 [2048, 128], replicated, may hold values from -0.01171875 to 0.01171875
- row_lse: bfloat16 [16384], P(('pair', 'dp')), may hold values from 6 to 9
- positive: int32 [16384], P(('pair', 'dp')), may hold values from 0 to 16383, as said below
Outputs:
- grad_embed: float32 [16384, 128], P(('pair', 'dp'))
- grad_weight: float32 [2048, 128], P('dp')
Inputs may be any that keep to these rules, and one draw needn't show every extreme that they name: positive[i] names the row that holds the other view of row i's cutout: positive[positive[i]] = i and positive[i] != i.
All inputs are finite; a program needn't handle non-finite values.
Results may differ from a plain program's by a relative error of at most 0.0045.
Values may be sent and summed in bfloat16 or wider, within the bound.
No kernel may reach another device: no remote copies, remote signals or barrier semaphores. Data moves between devices by JAX's collectives and lax.ppermute only.
A program may use at most 64 MiB of HBM per device.

v0:
```python
import jax
import jax.numpy as jnp
from jax import lax
from jax.sharding import PartitionSpec as P

contrastive_divisor = 0.1
epsilon = 1e-06


def from_behind(value, axis, steps):
    count = lax.axis_size(axis)
    pairs = [(source, (source + steps) % count) for source in range(count)]
    return lax.ppermute(value, axis, pairs)


def coupling_tile(embedded, own_lse, own_positive, counterpart_feature_vectors, part_lse, first_id):
    cosine_affinity_matrix = (
        lax.dot_general(
            embedded,
            counterpart_feature_vectors,
            (((1,), (1,)), ((), ())),
            preferred_element_type=jnp.float32,
        )
        / contrastive_divisor
    )
    weights = jnp.exp(cosine_affinity_matrix - own_lse.astype(jnp.float32)[:, None]) + jnp.exp(
        cosine_affinity_matrix - part_lse.astype(jnp.float32)[None, :]
    )
    identity_rows = first_id + jnp.arange(counterpart_feature_vectors.shape[0], dtype=jnp.int32)
    matched = (own_positive[:, None] == identity_rows[None, :]).astype(jnp.float32)
    return (weights - 2.0 * matched).astype(jnp.bfloat16)


def body(features, proj_weight, row_lse, positive):
    row_count = features.shape[0]
    dp_count = lax.axis_size("dp")
    pair_count = lax.axis_size("pair")
    group_rows = row_count * dp_count
    far_offset = pair_count // 4
    my_block = lax.axis_index("pair")
    projected = jnp.dot(features, proj_weight, preferred_element_type=jnp.float32)
    magnitude = jnp.sqrt(jnp.sum(projected * projected, axis=-1, keepdims=True) + epsilon)
    unit_vectors = projected / magnitude
    embedded = unit_vectors.astype(jnp.bfloat16)
    whole_embed, whole_lse = (
        lax.all_gather(embedded, "dp", axis=0, tiled=True),
        lax.all_gather(row_lse, "dp", axis=0, tiled=True),
    )
    upstream_derivative = jnp.zeros((row_count, embedded.shape[1]), jnp.float32)
    for offset in (1, far_offset):
        counterpart_feature_vectors, part_lse = from_behind(
            (whole_embed, whole_lse), "pair", offset
        )
        part_block = jnp.remainder(my_block - offset, pair_count)
        tile_coupling = coupling_tile(
            embedded,
            row_lse,
            positive,
            counterpart_feature_vectors,
            part_lse,
            part_block * group_rows,
        )
        coupling, counterpart_feature_vectors = (tile_coupling, counterpart_feature_vectors)
        upstream_derivative = upstream_derivative + jnp.dot(
            coupling, counterpart_feature_vectors, preferred_element_type=jnp.float32
        )
        returned = lax.psum_scatter(
            lax.dot_general(
                coupling, embedded, (((0,), (0,)), ((), ())), preferred_element_type=jnp.float32
            ),
            "dp",
            scatter_dimension=0,
            tiled=True,
        )
        upstream_derivative = upstream_derivative + from_behind(returned, "pair", -offset)
    derivative_pair_affinity = upstream_derivative / contrastive_divisor
    grad_embed = (
        derivative_pair_affinity
        - unit_vectors * jnp.sum(unit_vectors * derivative_pair_affinity, axis=-1, keepdims=True)
    ) / magnitude
    grad_half = grad_embed.astype(jnp.bfloat16)
    local_term = lax.dot_general(
        features, grad_half, (((0,), (0,)), ((), ())), preferred_element_type=jnp.float32
    )
    summed = lax.psum(local_term, "pair")
    grad_weight = lax.psum_scatter(summed, "dp", scatter_dimension=0, tiled=True)
    return (grad_embed, grad_weight)


def solution(mesh):
    return jax.shard_map(
        body,
        mesh=mesh,
        in_specs=(P(("pair", "dp"), None), P(), P(("pair", "dp")), P(("pair", "dp"))),
        out_specs=(P(("pair", "dp"), None), P("dp", None)),
        check_vma=False,
    )
```

profile of v0, /device:TPU:0, one launch (start us, length us, event | category | flops | bytes accessed | tf_op | source)
XLA Modules:
  0.0 204.0 jit_solution(16239086399272684663)
XLA Ops:
  7.2 1.5 copy-done
  8.8 1.9 multiply_reduce_fusion.1
  10.7 2.1 %all_gather.6 = bf16[1024,128]{0,1:T(8,128)(2,1)S(1)} all-gather(bf16[512,128]{0,1:T(8,128)(2,1)S(1)} %fusion.4), channel_id=1, replica_groups=mesh['pair'=16,'dp'=2] {'dp'}, dimensions={0}, use_global_device_ids=true | all-gather | bytes 393216 | tf_op jit(solution)/shard_map/all_gather | solution.py:46
  12.8 2.9 %collective-permute-start.3 = (bf16[1024,128]{0,1:T(8,128)(2,1)S(1)}, bf16[1024,128]{0,1:T(8,128)(2,1)S(1)}, u32[]{:S(2)}, u32[]{:S(2)}) collective-permute-start(bf16[1024,128]{0,1:T(8,128)(2,1)S(1)} %all_gather.6), channel_id=1, source_target_pairs={{0,8},{2,10},{4,12},{6,14},{8,16},{10,18},{12,20},{14,22},{16,24},... | collective-permute-start | bytes 786440 | tf_op jit(solution)/shard_map/ppermute | solution.py:13
  15.7 1.8 all-gather
  17.5 1.6 collective-permute-start.4
  19.2 1.5 collective-permute-start.1
  20.7 1.5 collective-permute-start
  22.1 2.3 %collective-permute-done.4 = bf16[1024]{0:T(1024)(128)(2,1)S(1)} collective-permute-done((bf16[1024]{0:T(1024)(128)(2,1)S(1)}, bf16[1024]{0:T(1024)(128)(2,1)S(1)}, u32[]{:S(2)}, u32[]{:S(2)}) %collective-permute-start.4) | collective-permute-done | bytes 2080 | tf_op jit(solution)/shard_map/ppermute | solution.py:13
  24.4 1.9 collective-permute-done.1
  26.8 5.3 %collective-permute-done = bf16[1024,128]{0,1:T(8,128)(2,1)S(1)} collective-permute-done((bf16[1024,128]{0,1:T(8,128)(2,1)S(1)}, bf16[1024,128]{0,1:T(8,128)(2,1)S(1)}, u32[]{:S(2)}, u32[]{:S(2)}) %collective-permute-start) | collective-permute-done | bytes 262176 | tf_op jit(solution)/shard_map/ppermute | solution.py:13
  32.8 3.0 %subtract_convert_fusion.1 = (bf16[512,1024]{1,0:T(8,128)(2,1)S(1)}, bf16[512,1024]{1,0:T(8,128)(2,1)S(1)}) fusion(s32[1024]{0:T(1024)S(1)} %get-tuple-element.15, f32[1024]{0:T(1024)S(1)} %convert_element_type.26, f32[512]{0:T(512)S(1)} %convert_element_type.25, s32[512]{0:T(512)S(1)} %copy-done.5, s32[1024]{0:T(1024)S(1)} %get-tuple-element.14, ...), kind=kOutput, calls=%fused_computation.2 | convolution fusion | flops 142606336 | bytes 4608000 | tf_op jit(solution)/shard_map/dot_general | solution.py:18
  37.9 1.1 fusion.7
  39.1 4.2 %reduce-scatter.6.cloned.1.call-done = f32[512,128]{0,1:T(8,128)} async-done(((f32[1024,128]{0,1:T(8,128)}), f32[512,128]{0,1:T(8,128)}) %reduce-scatter.6.cloned.1.call-update) | async-done | bytes 262160 | tf_op jit(solution)/shard_map/reduce_scatter | solution.py:67
  43.4 3.6 %collective-permute-start.5 = (f32[512,128]{0,1:T(8,128)}, f32[512,128]{0,1:T(8,128)}, u32[]{:S(2)}, u32[]{:S(2)}) collective-permute-start(f32[512,128]{0,1:T(8,128)} %reduce-scatter.6.cloned.1.call-done), channel_id=1, source_target_pairs={{0,24},{2,26},{4,28},{6,30},{8,0},{10,2},{12,4},{14,6},{16,8},{18,... | collective-permute-start | bytes 786440 | tf_op jit(solution)/shard_map/ppermute | solution.py:13
  46.9 7.9 %reduce-scatter.4.cloned.1.call-done = f32[512,128]{0,1:T(8,128)} async-done(((f32[1024,128]{0,1:T(8,128)}), f32[512,128]{0,1:T(8,128)}) %reduce-scatter.4.cloned.1.call-update) | async-done | bytes 262160 | tf_op jit(solution)/shard_map/reduce_scatter | solution.py:67
  54.8 5.4 %collective-permute-start.2 = (f32[512,128]{0,1:T(8,128)}, f32[512,128]{0,1:T(8,128)S(1)}, u32[]{:S(2)}, u32[]{:S(2)}) collective-permute-start(f32[512,128]{0,1:T(8,128)} %reduce-scatter.4.cloned.1.call-done), channel_id=1, source_target_pairs={{0,30},{2,0},{4,2},{6,4},{8,6},{10,8},{12,10},{14,12},{16,14},{18,... | collective-permute-start | bytes 786440 | tf_op jit(solution)/shard_map/ppermute | solution.py:13
  60.2 1.7 fusion.6
  62.0 4.6 %collective-permute-done.2 = f32[512,128]{0,1:T(8,128)S(1)} collective-permute-done((f32[512,128]{0,1:T(8,128)}, f32[512,128]{0,1:T(8,128)S(1)}, u32[]{:S(2)}, u32[]{:S(2)}) %collective-permute-start.2) | collective-permute-done | bytes 262176 | tf_op jit(solution)/shard_map/ppermute | solution.py:13
  66.6 1.6 multiply_reduce_fusion
  68.2 1.4 convolution_bitcast_fusion
  69.7 10.4 %reduce-scatter.8.cloned.1.call-done = f32[1024,128]{0,1:T(8,128)} async-done(((f32[2048,128]{0,1:T(8,128)}), f32[1024,128]{0,1:T(8,128)}) %reduce-scatter.8.cloned.1.call-update) | async-done | bytes 524304 | tf_op jit(solution)/shard_map/reduce_scatter | solution.py:86
  80.9 114.5 %all-reduce.2.cloned.1.call-done = f32[1024,128]{0,1:T(8,128)} async-done(((f32[1024,128]{0,1:T(8,128)}), f32[1024,128]{0,1:T(8,128)}) %all-reduce.2.cloned.1.call-update) | async-done | bytes 524304 | tf_op jit(solution)/shard_map/psum | solution.py:85
  195.4 2.0 copy.17
  (34 shorter events, 4.4 us)
Async XLA Ops:
  7.2 1.6 copy-start
  7.2 8.5 %copy-start.4 = (bf16[512]{0:T(512)(128)(2,1)S(1)}, bf16[512]{0:T(512)(128)(2,1)}, u32[]{:S(2)}) copy-start(bf16[512]{0:T(512)(128)(2,1)} %param.6) | copy-start | bytes 3076
  7.2 36.2 %reduce-scatter.6.cloned.1.call-start = ((), (), s32[]{:S(2)}) async-start(), calls=%async_computation.4 | async-start | bytes 786432 | tf_op jit(solution)/shard_map/reduce_scatter | solution.py:67
  10.6 22.2 %copy-start.5 = (s32[512]{0:T(512)S(1)}, s32[512]{0:T(512)}, u32[]{:S(2)}) copy-start(s32[512]{0:T(512)} %param.7) | copy-start | bytes 6148
  12.8 13.6 %collective-permute-start.3 = (bf16[1024,128]{0,1:T(8,128)(2,1)S(1)}, bf16[1024,128]{0,1:T(8,128)(2,1)S(1)}, u32[]{:S(2)}, u32[]{:S(2)}) collective-permute-start(bf16[1024,128]{0,1:T(8,128)(2,1)S(1)} %all_gather.6), channel_id=1, source_target_pairs={{0,8},{2,10},{4,12},{6,14},{8,16},{10,18},{12,20},{14,22},{16,24},... | collective-permute-start | bytes 786440 | tf_op jit(solution)/shard_map/ppermute | solution.py:13
  17.5 6.9 %collective-permute-start.4 = (bf16[1024]{0:T(1024)(128)(2,1)S(1)}, bf16[1024]{0:T(1024)(128)(2,1)S(1)}, u32[]{:S(2)}, u32[]{:S(2)}) collective-permute-start(bf16[1024]{0:T(1024)(128)(2,1)S(1)} %bitcast.20), channel_id=1, source_target_pairs={{0,8},{2,10},{4,12},{6,14},{8,16},{10,18},{12,20},{14,22},{16,24},... | collective-permute-start | bytes 6152 | tf_op jit(solution)/shard_map/ppermute | solution.py:13
  19.2 7.2 %collective-permute-start.1 = (bf16[1024]{0:T(1024)(128)(2,1)S(1)}, bf16[1024]{0:T(1024)(128)(2,1)S(1)}, u32[]{:S(2)}, u32[]{:S(2)}) collective-permute-start(bf16[1024]{0:T(1024)(128)(2,1)S(1)} %bitcast.21), channel_id=1, source_target_pairs={{0,2},{2,4},{4,6},{6,8},{8,10},{10,12},{12,14},{14,16},{16,18},{18... | collective-permute-start | bytes 6152 | tf_op jit(solution)/shard_map/ppermute | solution.py:13
  20.7 11.5 %collective-permute-start = (bf16[1024,128]{0,1:T(8,128)(2,1)S(1)}, bf16[1024,128]{0,1:T(8,128)(2,1)S(1)}, u32[]{:S(2)}, u32[]{:S(2)}) collective-permute-start(bf16[1024,128]{0,1:T(8,128)(2,1)S(1)} %all_gather.6), channel_id=1, source_target_pairs={{0,2},{2,4},{4,6},{6,8},{8,10},{10,12},{12,14},{14,16},{16,18},{18... | collective-permute-start | bytes 786440 | tf_op jit(solution)/shard_map/ppermute | solution.py:13
  26.3 5.8 %copy-start.2 = (bf16[1024,128]{0,1:T(8,128)(2,1)}, bf16[1024,128]{0,1:T(8,128)(2,1)S(1)}, u32[]{:S(2)}) copy-start(bf16[1024,128]{0,1:T(8,128)(2,1)S(1)} %collective-permute-done.3) | copy-start | bytes 786436
  32.1 0.7 copy-start.3
  35.8 1.0 copy-start.1
  37.9 17.0 %reduce-scatter.4.cloned.1.call-start = ((), (), s32[]{:S(2)}) async-start(), calls=%async_computation.3 | async-start | bytes 786432 | tf_op jit(solution)/shard_map/reduce_scatter | solution.py:67
  39.1 41.0 %reduce-scatter.8.cloned.1.call-start = ((), (), s32[]{:S(2)}) async-start(), calls=%async_computation.5 | async-start | bytes 1572864 | tf_op jit(solution)/shard_map/reduce_scatter | solution.py:86
  43.4 18.6 %collective-permute-start.5 = (f32[512,128]{0,1:T(8,128)}, f32[512,128]{0,1:T(8,128)}, u32[]{:S(2)}, u32[]{:S(2)}) collective-permute-start(f32[512,128]{0,1:T(8,128)} %reduce-scatter.6.cloned.1.call-done), channel_id=1, source_target_pairs={{0,24},{2,26},{4,28},{6,30},{8,0},{10,2},{12,4},{14,6},{16,8},{18,... | collective-permute-start | bytes 786440 | tf_op jit(solution)/shard_map/ppermute | solution.py:13
  54.8 11.7 %collective-permute-start.2 = (f32[512,128]{0,1:T(8,128)}, f32[512,128]{0,1:T(8,128)S(1)}, u32[]{:S(2)}, u32[]{:S(2)}) collective-permute-start(f32[512,128]{0,1:T(8,128)} %reduce-scatter.4.cloned.1.call-done), channel_id=1, source_target_pairs={{0,30},{2,0},{4,2},{6,4},{8,6},{10,8},{12,10},{14,12},{16,14},{18,... | collective-permute-start | bytes 786440 | tf_op jit(solution)/shard_map/ppermute | solution.py:13
  69.6 125.8 %all-reduce.2.cloned.1.call-start = ((), (), s32[]{:S(2)}) async-start(), calls=%async_computation.6 | async-start | bytes 1048576 | tf_op jit(solution)/shard_map/psum | solution.py:85
Sparse Core Ops, SparseCore 0:
  38.0 5.3 reduce-scatter.5
  45.7 9.1 reduce-scatter.3
  69.8 10.2 reduce-scatter.7
  85.9 109.4 all-reduce.1
where the time goes:
time: 204 us
  waiting for transfers between devices  151 us (74%)
  starting transfers between devices  16.6 us (8%)
  between operations  13.9 us (7%)
  matrix products  12.2 us (6%)
  local copies, waits for them, and re-layouts  6.09 us (3%)
  blocking collectives  3.86 us (2%)
    psum x1, waiting for transfers between devices, body(): summed = lax.psum(local_term, 'pair')  114 us
    ppermute x6, starting transfers between devices, from_behind(): return lax.ppermute(value, axis, pairs)  16.5 us
    ppermute x6, waiting for transfers between devices, from_behind(): return lax.ppermute(value, axis, pairs)  14.1 us
    reduce_scatter x2, waiting for transfers between devices, body(): lax.psum_scatter(lax.dot_general(coupling, embedded, (((0,), (0,)), ((),...  12.2 us
    reduce_scatter x1, waiting for transfers between devices, body(): lax.psum_scatter(summed, 'dp', scatter_dimension=0, tiled=True)  10.4 us
    unnamed x16, local copies, waits for them, and re-layouts  6.09 us
  transfers between devices with their start and end apart: 10, of which 8 were waited for; matrix products, arithmetic and copies ran while one was open for 2% of the time, Pallas kernels for 0%

commit v1 on v0

--- a/solution.py
+++ b/solution.py
@@ -82,7 +82,8 @@
     local_term = lax.dot_general(
         features, grad_half, (((0,), (0,)), ((), ())), preferred_element_type=jnp.float32
     )
-    summed = lax.psum(local_term, "pair")
+    parts = lax.all_gather(local_term, "pair", axis=0, tiled=False)
+    summed = parts.sum(axis=0)
     grad_weight = lax.psum_scatter(summed, "dp", scatter_dimension=0, tiled=True)
     return (grad_embed, grad_weight)
 

time: 204 us -> 308 us (1.51)
  waiting for transfers between devices: 151 us -> 226 us
  local copies, waits for them, and re-layouts: 6.09 us -> 23.8 us
  other arithmetic: 0.13 us -> 10.7 us
    all_gather x0 -> x1, waiting for transfers between devices: none -> 193 us  [body(): parts = lax.all_gather(local_term, 'pair', axis=0, tiled=False)]
    psum x1 -> x0, waiting for transfers between devices: 114 us -> none  [body(): summed = lax.psum(local_term, 'pair')]
    unnamed x16 -> x17, local copies, waits for them, and re-layouts: 6.09 us -> 23.8 us
    reduce_sum x0 -> x1, other arithmetic: none -> 10.6 us  [body(): summed = parts.sum(axis=0)]
    reduce_scatter x1, waiting for transfers between devices: 10.4 us -> 7.01 us  [body(): lax.psum_scatter(summed, 'dp', scatter_dimension=0, tiled=True)]
  transfers between devices with their start and end apart: 10 -> 10, of which waited for: 8 -> 8; matrix products, arithmetic and copies ran while one was open for 2% -> 1% of each run, Pallas kernels for 0% -> 0%
where the time goes in v1:
time: 308 us; the launch traced here: 307 us
  waiting for transfers between devices  226 us (73%)
  local copies, waits for them, and re-layouts  23.8 us (8%)
  starting transfers between devices  16.8 us (5%)
  between operations  13.9 us (5%)
  matrix products  12.3 us (4%)
  other arithmetic  10.7 us (3%)
  blocking collectives  3.85 us (1%)
    all_gather x1, waiting for transfers between devices, body(): parts = lax.all_gather(local_term, 'pair', axis=0, tiled=False)  193 us
    unnamed x17, local copies, waits for them, and re-layouts  23.8 us
    ppermute x6, starting transfers between devices, from_behind(): return lax.ppermute(value, axis, pairs)  16.5 us
    ppermute x6, waiting for transfers between devices, from_behind(): return lax.ppermute(value, axis, pairs)  14.1 us
    reduce_scatter x2, waiting for transfers between devices, body(): lax.psum_scatter(lax.dot_general(coupling, embedded, (((0,), (0,)), ((),...  12.1 us
    reduce_sum x1, other arithmetic, body(): summed = parts.sum(axis=0)  10.6 us
    reduce_scatter x1, waiting for transfers between devices, body(): lax.psum_scatter(summed, 'dp', scatter_dimension=0, tiled=True)  7.01 us
  transfers between devices with their start and end apart: 10, of which 8 were waited for; matrix products, arithmetic and copies ran while one was open for 1% of the time, Pallas kernels for 0%

profile of v1, /device:TPU:0, one launch (start us, length us, event | category | flops | bytes accessed | tf_op | source)
XLA Modules:
  0.0 307.3 jit_solution(11187594088524713232)
XLA Ops:
  7.2 1.5 copy-done
  8.8 1.9 multiply_reduce_fusion.1
  10.7 2.1 all_gather.12
  12.8 2.9 collective-permute-start.3
  15.7 1.8 all-gather.1
  17.5 1.6 collective-permute-start.4
  19.2 1.5 collective-permute-start.1
  20.7 1.5 collective-permute-start
  22.1 2.3 collective-permute-done.4
  24.4 1.9 collective-permute-done.1
  26.8 5.3 %collective-permute-done = bf16[1024,128]{0,1:T(8,128)(2,1)S(1)} collective-permute-done((bf16[1024,128]{0,1:T(8,128)(2,1)S(1)}, bf16[1024,128]{0,1:T(8,128)(2,1)S(1)}, u32[]{:S(2)}, u32[]{:S(2)}) %collective-permute-start) | collective-permute-done | bytes 262176 | tf_op jit(solution)/shard_map/ppermute | solution.py:13
  32.8 3.0 subtract_convert_fusion.1
  39.1 4.2 %reduce-scatter.6.cloned.1.call-done = f32[512,128]{0,1:T(8,128)} async-done(((f32[1024,128]{0,1:T(8,128)}), f32[512,128]{0,1:T(8,128)}) %reduce-scatter.6.cloned.1.call-update) | async-done | bytes 262160 | tf_op jit(solution)/shard_map/reduce_scatter | solution.py:67
  43.4 3.6 %collective-permute-start.5 = (f32[512,128]{0,1:T(8,128)}, f32[512,128]{0,1:T(8,128)}, u32[]{:S(2)}, u32[]{:S(2)}) collective-permute-start(f32[512,128]{0,1:T(8,128)} %reduce-scatter.6.cloned.1.call-done), channel_id=1, source_target_pairs={{0,24},{2,26},{4,28},{6,30},{8,0},{10,2},{12,4},{14,6},{16,8},{18,... | collective-permute-start | bytes 786440 | tf_op jit(solution)/shard_map/ppermute | solution.py:13
  46.9 7.9 %reduce-scatter.4.cloned.1.call-done = f32[512,128]{0,1:T(8,128)} async-done(((f32[1024,128]{0,1:T(8,128)}), f32[512,128]{0,1:T(8,128)}) %reduce-scatter.4.cloned.1.call-update) | async-done | bytes 262160 | tf_op jit(solution)/shard_map/reduce_scatter | solution.py:67
  54.8 5.4 %collective-permute-start.2 = (f32[512,128]{0,1:T(8,128)}, f32[512,128]{0,1:T(8,128)S(1)}, u32[]{:S(2)}, u32[]{:S(2)}) collective-permute-start(f32[512,128]{0,1:T(8,128)} %reduce-scatter.4.cloned.1.call-done), channel_id=1, source_target_pairs={{0,30},{2,0},{4,2},{6,4},{8,6},{10,8},{12,10},{14,12},{16,14},{18,... | collective-permute-start | bytes 786440 | tf_op jit(solution)/shard_map/ppermute | solution.py:13
  60.2 1.7 fusion.6
  62.0 4.6 %collective-permute-done.2 = f32[512,128]{0,1:T(8,128)S(1)} collective-permute-done((f32[512,128]{0,1:T(8,128)}, f32[512,128]{0,1:T(8,128)S(1)}, u32[]{:S(2)}, u32[]{:S(2)}) %collective-permute-start.2) | collective-permute-done | bytes 262176 | tf_op jit(solution)/shard_map/ppermute | solution.py:13
  66.6 1.6 multiply_reduce_fusion
  69.9 192.7 %all-gather.4.cloned.1.call-done = f32[32768,128]{0,1:T(8,128)} async-done(((f32[2048,128]{0,1:T(8,128)}), f32[32768,128]{0,1:T(8,128)}) %all-gather.4.cloned.1.call-update) | async-done | bytes 16777232 | tf_op jit(solution)/shard_map/all_gather | solution.py:85
  262.6 17.7 %copy.19 = f32[16,8,16,2048]{3,2,1,0:T(8,128)} copy(f32[16,8,16,2048]{3,1,2,0:T(8,128)} %bitcast.24) | data formatting | bytes 33554432
  280.3 10.6 %bitcast_reduce_fusion = f32[2048,128]{0,1:T(8,128)} fusion(f32[16,8,16,2048]{3,2,1,0:T(8,128)} %copy.19), kind=kLoop, calls=%fused_computation | loop fusion | flops 3932160 | bytes 17825792 | tf_op jit(solution)/shard_map/reduce_sum | solution.py:86
  291.8 7.0 %reduce-scatter.8.cloned.1.call-done = f32[1024,128]{0,1:T(8,128)} async-done(((f32[2048,128]{0,1:T(8,128)}), f32[1024,128]{0,1:T(8,128)}) %reduce-scatter.8.cloned.1.call-update) | async-done | bytes 524304 | tf_op jit(solution)/shard_map/reduce_scatter | solution.py:87
  298.8 2.0 copy.15
  (36 shorter events, 7.2 us)
Async XLA Ops:
  7.2 1.6 copy-start
  7.2 8.5 %copy-start.4 = (bf16[512]{0:T(512)(128)(2,1)S(1)}, bf16[512]{0:T(512)(128)(2,1)}, u32[]{:S(2)}) copy-start(bf16[512]{0:T(512)(128)(2,1)} %param.6) | copy-start | bytes 3076
  7.2 36.2 %reduce-scatter.6.cloned.1.call-start = ((), (), s32[]{:S(2)}) async-start(), calls=%async_computation.4 | async-start | bytes 786432 | tf_op jit(solution)/shard_map/reduce_scatter | solution.py:67
  10.6 22.2 %copy-start.5 = (s32[512]{0:T(512)S(1)}, s32[512]{0:T(512)}, u32[]{:S(2)}) copy-start(s32[512]{0:T(512)} %param.7) | copy-start | bytes 6148
  12.8 13.6 %collective-permute-start.3 = (bf16[1024,128]{0,1:T(8,128)(2,1)S(1)}, bf16[1024,128]{0,1:T(8,128)(2,1)S(1)}, u32[]{:S(2)}, u32[]{:S(2)}) collective-permute-start(bf16[1024,128]{0,1:T(8,128)(2,1)S(1)} %all_gather.12), channel_id=1, source_target_pairs={{0,8},{2,10},{4,12},{6,14},{8,16},{10,18},{12,20},{14,22},{16,24},... | collective-permute-start | bytes 786440 | tf_op jit(solution)/shard_map/ppermute | solution.py:13
  17.5 6.9 %collective-permute-start.4 = (bf16[1024]{0:T(1024)(128)(2,1)S(1)}, bf16[1024]{0:T(1024)(128)(2,1)S(1)}, u32[]{:S(2)}, u32[]{:S(2)}) collective-permute-start(bf16[1024]{0:T(1024)(128)(2,1)S(1)} %bitcast.26), channel_id=1, source_target_pairs={{0,8},{2,10},{4,12},{6,14},{8,16},{10,18},{12,20},{14,22},{16,24},... | collective-permute-start | bytes 6152 | tf_op jit(solution)/shard_map/ppermute | solution.py:13
  19.2 7.2 %collective-permute-start.1 = (bf16[1024]{0:T(1024)(128)(2,1)S(1)}, bf16[1024]{0:T(1024)(128)(2,1)S(1)}, u32[]{:S(2)}, u32[]{:S(2)}) collective-permute-start(bf16[1024]{0:T(1024)(128)(2,1)S(1)} %bitcast.27), channel_id=1, source_target_pairs={{0,2},{2,4},{4,6},{6,8},{8,10},{10,12},{12,14},{14,16},{16,18},{18... | collective-permute-start | bytes 6152 | tf_op jit(solution)/shard_map/ppermute | solution.py:13
  20.7 11.5 %collective-permute-start = (bf16[1024,128]{0,1:T(8,128)(2,1)S(1)}, bf16[1024,128]{0,1:T(8,128)(2,1)S(1)}, u32[]{:S(2)}, u32[]{:S(2)}) collective-permute-start(bf16[1024,128]{0,1:T(8,128)(2,1)S(1)} %all_gather.12), channel_id=1, source_target_pairs={{0,2},{2,4},{4,6},{6,8},{8,10},{10,12},{12,14},{14,16},{16,18},{18... | collective-permute-start | bytes 786440 | tf_op jit(solution)/shard_map/ppermute | solution.py:13
  26.3 5.8 %copy-start.2 = (bf16[1024,128]{0,1:T(8,128)(2,1)}, bf16[1024,128]{0,1:T(8,128)(2,1)S(1)}, u32[]{:S(2)}) copy-start(bf16[1024,128]{0,1:T(8,128)(2,1)S(1)} %collective-permute-done.3) | copy-start | bytes 786436
  32.1 0.7 copy-start.3
  35.8 1.0 copy-start.1
  37.9 16.9 %reduce-scatter.4.cloned.1.call-start = ((), (), s32[]{:S(2)}) async-start(), calls=%async_computation.3 | async-start | bytes 786432 | tf_op jit(solution)/shard_map/reduce_scatter | solution.py:67
  39.1 223.5 %all-gather.4.cloned.1.call-start = ((), (), s32[]{:S(2)}) async-start(), calls=%async_computation.6 | async-start | bytes 17825792 | tf_op jit(solution)/shard_map/all_gather | solution.py:85
  43.4 18.6 %collective-permute-start.5 = (f32[512,128]{0,1:T(8,128)}, f32[512,128]{0,1:T(8,128)}, u32[]{:S(2)}, u32[]{:S(2)}) collective-permute-start(f32[512,128]{0,1:T(8,128)} %reduce-scatter.6.cloned.1.call-done), channel_id=1, source_target_pairs={{0,24},{2,26},{4,28},{6,30},{8,0},{10,2},{12,4},{14,6},{16,8},{18,... | collective-permute-start | bytes 786440 | tf_op jit(solution)/shard_map/ppermute | solution.py:13
  54.8 11.8 %collective-permute-start.2 = (f32[512,128]{0,1:T(8,128)}, f32[512,128]{0,1:T(8,128)S(1)}, u32[]{:S(2)}, u32[]{:S(2)}) collective-permute-start(f32[512,128]{0,1:T(8,128)} %reduce-scatter.4.cloned.1.call-done), channel_id=1, source_target_pairs={{0,30},{2,0},{4,2},{6,4},{8,6},{10,8},{12,10},{14,12},{16,14},{18,... | collective-permute-start | bytes 786440 | tf_op jit(solution)/shard_map/ppermute | solution.py:13
  69.6 229.1 %reduce-scatter.8.cloned.1.call-start = ((), (), s32[]{:S(2)}) async-start(), calls=%async_computation.5 | async-start | bytes 1572864 | tf_op jit(solution)/shard_map/reduce_scatter | solution.py:87
Sparse Core Ops, SparseCore 0:
  38.0 5.3 reduce-scatter.5
  45.7 9.0 reduce-scatter.3
  69.8 192.8 all-gather.3
  291.0 7.6 reduce-scatter.7
